TPU v7x, 32 devices: a whole 2x2x4 slice. The times are simulated.
32 devices in a mesh: ctx: 8 (over z, x), tp: 4 (over y, core).
Axes of the slice: x: 2, y: 2, z: 4, core: 2. Of those that a mesh axis runs over, the one named last changes fastest.
Arguments:
- q_nope: bfloat16 [8, 128, 128], P('ctx', 'tp'), may hold values from -6 to 6
- q_rope: bfloat16 [8, 128, 64], P('ctx', 'tp'), may hold values from -256 to 256
- w_uk: bfloat16 [128, 128, 512], P('tp'), may hold values from -0.5 to 0.5
- w_uv: bfloat16 [128, 512, 128], P('tp'), may hold values from -3 to 3
- w_out: bfloat16 [16384, 7168], P('tp', 'ctx'), may hold values from -0.046875 to 0.046875
- prefix_cache: bfloat16 [32768, 576], P('ctx'), may hold values from -6 to 6
- block_table: int32 [512], P('ctx'), may hold values from 0 to 511, each once
- prefix_len: int32 [8], replicated, may hold values from 8192 to 32768
- suffix_cache: bfloat16 [8, 256, 576], P('ctx'), may hold values from -12 to 12
- suffix_len: int32 [8], P('ctx'), may hold values from 2 to 256
Outputs:
- layer_out: bfloat16 [8, 7168], P('tp', 'ctx')
Inputs may be any that keep to these rules, and one draw needn't show every extreme that they name: A permutation: slots b * 64 to b * 64 + 63 of prefix_cache hold prefix positions block_table[b] * 64 onwards.
All inputs are finite; a program needn't handle non-finite values.
Results may differ from a plain program's by a relative error of at most 0.0078.
Values may be sent and summed in bfloat16 or wider, within the bound.
A program may use at most 64 MiB of HBM per device.

v0:
```python
import jax
import jax.numpy as jnp
from jax import lax
from jax.sharding import PartitionSpec as P

LAT = 512
ROPE = 64
NOPE = 128
BLOCK = 64
masked_value = -1e30


def partial_stats(scores, visible, values, pattern):
    row_peak = jnp.max(jnp.where(visible, scores, masked_value), axis=2)
    weights = jnp.where(visible, jnp.exp(scores - row_peak[:, :, None]), 0.0).astype(jnp.bfloat16)
    row_mass = jnp.sum(weights, axis=2, dtype=jnp.float32)
    row_weighted = jnp.einsum(pattern, weights, values, preferred_element_type=jnp.float32)
    return (row_peak, row_mass, row_weighted)


def value_project(latent, value_weight):
    return jnp.einsum("rhc,hcv->rhv", latent, value_weight, precision=lax.Precision.HIGHEST)


def on_device(
    q_nope,
    q_rope,
    w_uk,
    w_uv,
    w_out,
    prefix_cache,
    block_table,
    prefix_len,
    suffix_cache,
    suffix_len,
):
    softmax_scale = (NOPE + ROPE) ** (-0.5)
    q_latent = jnp.einsum("rhn,hnc->rhc", q_nope, w_uk, preferred_element_type=jnp.float32).astype(
        jnp.bfloat16
    )
    own_queries = jnp.concatenate([q_latent, q_rope], axis=2)
    all_queries = lax.all_gather(own_queries, "ctx", axis=0, tiled=True)
    ctx_count = lax.axis_size("ctx")
    own_count = own_queries.shape[0]
    value_weight = w_uv.astype(jnp.float32)
    positions = (
        block_table[:, None] * BLOCK + jnp.arange(BLOCK, dtype=jnp.int32)[None, :]
    ).reshape(-1)
    visible = (positions[None, :] < prefix_len[:, None])[:, None, :]
    scores = (
        jnp.einsum("rhc,tc->rht", all_queries, prefix_cache, preferred_element_type=jnp.float32)
        * softmax_scale
    )
    row_peak, row_mass, row_weighted = partial_stats(
        scores, visible, prefix_cache[:, :LAT], "rht,tc->rhc"
    )
    suffix_scores = (
        jnp.einsum("rhc,rtc->rht", own_queries, suffix_cache, preferred_element_type=jnp.float32)
        * softmax_scale
    )
    suffix_slots = jnp.arange(suffix_cache.shape[1], dtype=jnp.int32)
    suffix_visible = (suffix_slots[None, :] < suffix_len[:, None])[:, None, :]
    tail_peak, tail_mass, tail_weighted = partial_stats(
        suffix_scores, suffix_visible, suffix_cache[:, :, :LAT], "rht,rtc->rhc"
    )

    def by_owner(values):
        return values.reshape((ctx_count, own_count) + values.shape[1:])

    got_peak, got_mass, got_weighted = (
        lax.all_to_all(by_owner(row_peak), "ctx", split_axis=0, concat_axis=0, tiled=True),
        lax.all_to_all(by_owner(row_mass), "ctx", split_axis=0, concat_axis=0, tiled=True),
        lax.all_to_all(by_owner(row_weighted), "ctx", split_axis=0, concat_axis=0, tiled=True),
    )
    highest = jnp.maximum(jnp.max(got_peak, axis=0), tail_peak)
    factors = jnp.exp(got_peak - highest[None])
    tail_factor = jnp.exp(tail_peak - highest)
    total_mass = jnp.sum(factors * got_mass, axis=0) + tail_factor * tail_mass
    total_weighted = (
        jnp.sum(factors[..., None] * got_weighted, axis=0) + tail_factor[:, :, None] * tail_weighted
    )
    head_values = value_project(total_weighted / total_mass[:, :, None], value_weight).astype(
        jnp.bfloat16
    )
    flat_values = head_values.reshape(own_count, -1)
    every_value = lax.all_gather(flat_values, "ctx", axis=0, tiled=True)
    return lax.psum_scatter(
        jnp.dot(every_value, w_out, preferred_element_type=jnp.float32),
        "tp",
        scatter_dimension=0,
        tiled=True,
    ).astype(jnp.bfloat16)


def solution(mesh):
    placed = (
        P("ctx", "tp", None),
        P("ctx", "tp", None),
        P("tp", None, None),
        P("tp", None, None),
        P("tp", "ctx"),
        P("ctx", None),
        P("ctx"),
        P(),
        P("ctx", None, None),
        P("ctx"),
    )
    return jax.shard_map(
        on_device, mesh=mesh, in_specs=placed, out_specs=P("tp", "ctx"), check_vma=False
    )
```

profile of v0, /device:TPU:0, one launch (start us, length us, event | category | flops | bytes accessed | tf_op | source)
XLA Modules:
  0.0 129.5 jit_solution(10840114998855403633)
XLA Ops:
  0.0 0.0 copy-start
  0.0 0.0 copy-start.3
  0.0 0.0 copy-start.4
  0.0 0.7 broadcast_multiply_fusion
  0.7 0.1 iota_add_fusion
  0.8 0.1 add.38
  0.9 0.0 copy-done
  0.9 0.0 copy-start.5
  0.9 3.0 %fusion.20 = bf16[32,1,512]{2,1,0:T(2,128)(2,1)S(1)} fusion(bf16[32,128,512]{2,1,0:T(8,128)(2,1)} %param.12, bf16[32,128,1]{1,0,2:T(8,128)(2,1)S(1)} %bitcast.55), kind=kOutput, calls=%fused_computation.32 | convolution fusion | flops 4194304 | bytes 4235264 | tf_op jit(solution)/shard_map/rhn,hnc->rhc/dot_general | solution.py:38
  3.9 0.0 copy-done.3
  3.9 32.7 %all_gather.6 = bf16[8,32,576]{2,1,0:T(8,128)(2,1)S(1)} all-gather(bf16[1,32,576]{2,1,0:T(8,128)(2,1)S(1)} %pad_maximum_fusion), channel_id=1, replica_groups=mesh['ctx'=8,'tp'=4] {'ctx'}, dimensions={0}, use_global_device_ids=true | all-gather | bytes 331776 | tf_op jit(solution)/shard_map/all_gather | solution.py:42
  36.6 0.0 copy-done.4
  36.6 0.1 broadcast_compare_fusion
  36.7 0.0 copy-done.5
  36.7 2.7 %select_reduce_fusion = (f32[8,32]{1,0:T(8,128)}, f32[8,32,4096]{2,1,0:T(8,128)S(1)}) fusion(pred[8,4096]{1,0:T(8,128)(4,1)S(1)} %broadcast_compare_fusion, bf16[8,32,576]{2,1,0:T(8,128)(2,1)S(1)} %all_gather.6, bf16[4096,576]{0,1:T(8,128)(2,1)S(1)} %copy-done.5), kind=kOutput, calls=%fused_computation.7 | convolution fusion | flops 1211105024 | bytes 9241600 | tf_op jit(solution)/shard_map/rhc,tc->rht/dot_general | solution.py:51
  39.4 0.0 copy-start.1
  39.4 1.9 %copy-done.1 = f32[8,32,4096]{2,1,0:T(8,128)} copy-done((f32[8,32,4096]{2,1,0:T(8,128)}, f32[8,32,4096]{2,1,0:T(8,128)S(1)}, u32[]{:S(2)}) %copy-start.1) | copy-done | bytes 4194328
  41.3 1.7 %convert_reduce_fusion = f32[8,32]{1,0:T(8,128)S(1)} fusion(f32[8,32,4096]{2,1,0:T(8,128)S(1)} %get-tuple-element.10, f32[8,32]{1,0:T(8,128)} %get-tuple-element.9, pred[8,4096]{1,0:T(8,128)(4,1)S(1)} %broadcast_compare_fusion), kind=kLoop, calls=%fused_computation.4 | loop fusion | flops 5242624 | bytes 4229120 | tf_op jit(solution)/shard_map/reduce_sum | solution.py:16
  43.0 11.8 %all_to_all.15 = f32[8,1,32]{2,1,0:T(1,128)S(1)} all-to-all(f32[8,1,32]{2,1,0:T(1,128)S(1)} %bitcast.60), channel_id=1, replica_groups=mesh['ctx'=8,'tp'=4] {'ctx'}, dimensions={0} | all-to-all | bytes 2048 | tf_op jit(solution)/shard_map/all_to_all | solution.py:72
  54.9 3.2 %all-to-all-start = ((f32[8,1,32]{2,1,0:T(1,128)}), f32[8,1,32]{2,1,0:T(1,128)S(1)}, u32[]{:S(2)}, u32[]{:S(2)}) async-start(f32[8,1,32]{2,1,0:T(1,128)} %bitcast.5), calls=%async_computation | async-start | bytes 8192 | tf_op jit(solution)/shard_map/all_to_all | solution.py:71
  58.1 0.0 copy-start.6
  58.1 0.0 copy-start.2
  58.1 5.6 %fusion.4 = f32[8,1,32,512]{3,2,1,0:T(8,128)} fusion(bf16[4096,576]{0,1:T(8,128)(2,1)} %param.15, f32[8,32,4096]{2,1,0:T(8,128)} %copy-done.1, f32[8,32]{1,0:T(8,128)} %get-tuple-element.9, pred[8,4096]{1,0:T(8,128)(4,1)S(1)} %broadcast_compare_fusion), kind=kOutput, calls=%fused_computation.8 | convolution fusion | flops 1076887552 | bytes 8949760 | tf_op jit(solution)/shard_map/rht,tc->rhc/dot_general | solution.py:17
  63.7 0.8 all-to-all-done
  64.5 5.1 %all-to-all-start.1 = ((f32[8,1,32,512]{3,2,1,0:T(8,128)}), f32[8,1,32,512]{3,2,1,0:T(8,128)S(1)}, u32[]{:S(2)}, u32[]{:S(2)}) async-start(f32[8,1,32,512]{3,2,1,0:T(8,128)} %fusion.4), calls=%async_computation.1 | async-start | bytes 1048576 | tf_op jit(solution)/shard_map/all_to_all | solution.py:73
  70.3 0.0 copy-done.6
  70.3 0.7 dynamic-slice
  71.7 0.0 copy-done.2
  71.7 0.3 select_reduce_fusion.1
  72.0 0.2 convert_reduce_fusion.1
  72.2 7.8 %all-to-all-done.1 = f32[8,1,32,512]{3,2,1,0:T(8,128)S(1)} async-done(((f32[8,1,32,512]{3,2,1,0:T(8,128)}), f32[8,1,32,512]{3,2,1,0:T(8,128)S(1)}, u32[]{:S(2)}, u32[]{:S(2)}) %all-to-all-start.1) | async-done | bytes 524320 | tf_op jit(solution)/shard_map/all_to_all | solution.py:73
  80.0 0.1 multiply_reduce_fusion
  80.1 0.2 fusion.9
  80.3 3.5 %fusion.16 = f32[32,1,128]{2,1,0:T(1,128)S(1)} fusion(bf16[32,512,128]{2,1,0:T(8,128)(2,1)} %param.13, f32[32,512,1]{1,0,2:T(8,128)S(1)} %fusion.9), kind=kOutput, calls=%fused_computation.22 | convolution fusion | flops 25165824 | bytes 4276224 | tf_op jit(solution)/shard_map/rhc,hcv->rhv/dot_general | solution.py:22
  83.9 30.5 %all-gather = bf16[8,1,4096]{2,1,0:T(2,128)(2,1)S(1)} all-gather(bf16[1,1,4096]{2,1,0:T(2,128)(2,1)S(1)} %reshape.166), channel_id=1, replica_groups=mesh['ctx'=8,'tp'=4] {'ctx'}, dimensions={0}, use_global_device_ids=true | all-gather | bytes 73728 | tf_op jit(solution)/shard_map/all_gather | solution.py:86
  114.4 4.1 %fusion.13 = f32[8,896]{1,0:T(8,128)S(1)} fusion(bf16[4096,896]{1,0:T(8,128)(2,1)} %param.14, bf16[8,1,4096]{2,1,0:T(2,128)(2,1)S(1)} %all-gather), kind=kOutput, calls=%fused_computation.18 | convolution fusion | flops 58720256 | bytes 7434240 | tf_op jit(solution)/shard_map/dot_general | solution.py:88
  118.6 10.3 %all-reduce = bf16[8,896]{1,0:T(8,128)(2,1)S(1)} all-reduce(f32[8,896]{1,0:T(8,128)S(1)} %fusion.13), channel_id=2, replica_groups=mesh['ctx'=8,'tp'=4] {'tp'}, use_global_device_ids=true, to_apply=%region_7.8.clone | all-reduce | flops 7168 | bytes 43008
  128.9 0.6 dynamic-slice_convert_fusion
  (9 shorter events, 0.1 us)
Async XLA Ops:
  0.0 0.9 copy-start
  0.0 3.9 %copy-start.3 = (bf16[1,32,64]{2,1,0:T(8,128)(2,1)S(1)}, bf16[1,32,64]{2,1,0:T(8,128)(2,1)}, u32[]{:S(2)}) copy-start(bf16[1,32,64]{2,1,0:T(8,128)(2,1)} %param.11) | copy-start | bytes 12292
  0.0 36.6 %copy-start.4 = (s32[8]{0:T(128)S(1)}, s32[8]{0:T(128)}, u32[]{:S(2)}) copy-start(s32[8]{0:T(128)} %param.17) | copy-start | bytes 100
  0.9 35.8 %copy-start.5 = (bf16[4096,576]{0,1:T(8,128)(2,1)S(1)}, bf16[4096,576]{0,1:T(8,128)(2,1)}, u32[]{:S(2)}) copy-start(bf16[4096,576]{0,1:T(8,128)(2,1)} %param.15) | copy-start | bytes 14155780
  39.4 1.9 %copy-start.1 = (f32[8,32,4096]{2,1,0:T(8,128)}, f32[8,32,4096]{2,1,0:T(8,128)S(1)}, u32[]{:S(2)}) copy-start(f32[8,32,4096]{2,1,0:T(8,128)S(1)} %get-tuple-element.10) | copy-start | bytes 12582916
  54.9 9.7 %all-to-all-start = ((f32[8,1,32]{2,1,0:T(1,128)}), f32[8,1,32]{2,1,0:T(1,128)S(1)}, u32[]{:S(2)}, u32[]{:S(2)}) async-start(f32[8,1,32]{2,1,0:T(1,128)} %bitcast.5), calls=%async_computation | async-start | bytes 8192 | tf_op jit(solution)/shard_map/all_to_all | solution.py:71
  58.1 12.2 %copy-start.6 = (u32[32]{0:T(128)S(1)}, u32[32]{0:T(128)}, u32[]{:S(2)}) copy-start(u32[32]{0:T(128)} %constant.17) | copy-start | bytes 388
  58.1 13.6 %copy-start.2 = (bf16[1,256,576]{1,2,0:T(8,128)(2,1)S(1)}, bf16[1,256,576]{1,2,0:T(8,128)(2,1)}, u32[]{:S(2)}) copy-start(bf16[1,256,576]{1,2,0:T(8,128)(2,1)} %param.18) | copy-start | bytes 884740
  64.5 15.5 %all-to-all-start.1 = ((f32[8,1,32,512]{3,2,1,0:T(8,128)}), f32[8,1,32,512]{3,2,1,0:T(8,128)S(1)}, u32[]{:S(2)}, u32[]{:S(2)}) async-start(f32[8,1,32,512]{3,2,1,0:T(8,128)} %fusion.4), calls=%async_computation.1 | async-start | bytes 1048576 | tf_op jit(solution)/shard_map/all_to_all | solution.py:73
where the time goes:
time: 130 us; the launch traced here: 129 us
  blocking collectives  85.4 us (66%)
  matrix products  19.4 us (15%)
  waiting for transfers between devices  8.58 us (7%)
  starting transfers between devices  8.34 us (6%)
  local copies, waits for them, and re-layouts  3.31 us (3%)
  other arithmetic  3 us (2%)
  between operations  1.49 us (1%)
    all_gather x1, blocking collectives, on_device(): all_queries = lax.all_gather(own_queries, 'ctx', axis=0, tiled=True)  32.7 us
    all_gather x1, blocking collectives, on_device(): every_value = lax.all_gather(flat_values, 'ctx', axis=0, tiled=True)  30.5 us
    all_to_all x1, blocking collectives, on_device(): lax.all_to_all(by_owner(row_mass), 'ctx', split_axis=0, concat_axis=0, ti...  11.8 us
    unnamed x1, blocking collectives  10.3 us
    all_to_all x1, waiting for transfers between devices, on_device(): lax.all_to_all(by_owner(row_weighted), 'ctx', split_axis=0, concat_axis=0...  7.78 us
    dot_general x2, matrix products, partial_stats(): jnp.einsum(pattern, weights, values, preferred_element_type=jnp.float32)  5.81 us
    all_to_all x1, starting transfers between devices, on_device(): lax.all_to_all(by_owner(row_weighted), 'ctx', split_axis=0, concat_axis=0...  5.12 us
    dot_general x1, matrix products, on_device(): jnp.dot(every_value, w_out, preferred_element_type=jnp.float32)  4.14 us
  transfers between devices with their start and end apart: 2, of which 2 were waited for; matrix products, arithmetic and copies ran while one was open for 5% of the time, Pallas kernels for 0%

commit v1 on v0

--- a/solution.py
+++ b/solution.py
@@ -8,6 +8,28 @@
 NOPE = 128
 BLOCK = 64
 masked_value = -1e30
+
+
+def _cut_local_data(row_data, link_axis, array_axis, a0, axis_no):
+    tmp = lax.axis_size(link_axis)
+    piece_out = lax.axis_index(link_axis)
+    val, raw_out, reply = (tmp, piece_out, row_data.shape[array_axis])
+    u1, piece_now = ([], [])
+    arr_next = oldest = row_data
+    for u in range(val // 2 + 1):
+        u1.append(a0(arr_next, (raw_out - u) % val * reply))
+        if 0 < u < val - val // 2:
+            piece_now.append(a0(oldest, (raw_out + u) % val * reply))
+        ledger = []
+        for ix in range(val):
+            ledger.append((ix, (ix + 1) % val))
+        arr_next = lax.ppermute(arr_next, link_axis, ledger)
+        panels = []
+        for ix in range(val):
+            panels.append((ix, (ix - 1) % val))
+        oldest = lax.ppermute(oldest, axis_name=link_axis, perm=panels)
+    outer = jnp.concatenate([*u1[::-1], *piece_now], axis=axis_no)
+    return jnp.roll(outer, (raw_out - val // 2) * u1[0].shape[axis_no], axis=axis_no)
 
 
 def partial_stats(scores, visible, values, pattern):
@@ -39,7 +61,6 @@
         jnp.bfloat16
     )
     own_queries = jnp.concatenate([q_latent, q_rope], axis=2)
-    all_queries = lax.all_gather(own_queries, "ctx", axis=0, tiled=True)
     ctx_count = lax.axis_size("ctx")
     own_count = own_queries.shape[0]
     value_weight = w_uv.astype(jnp.float32)
@@ -48,7 +69,15 @@
     ).reshape(-1)
     visible = (positions[None, :] < prefix_len[:, None])[:, None, :]
     scores = (
-        jnp.einsum("rhc,tc->rht", all_queries, prefix_cache, preferred_element_type=jnp.float32)
+        _cut_local_data(
+            own_queries,
+            "ctx",
+            0,
+            lambda part, offset: jnp.einsum(
+                "rhc,tc->rht", part, prefix_cache, preferred_element_type=jnp.float32
+            ),
+            0,
+        )
         * softmax_scale
     )
     row_peak, row_mass, row_weighted = partial_stats(

time: 130 us -> 132 us (1.015)
  blocking collectives: 85.4 us -> 49.7 us
  starting transfers between devices: 8.34 us -> 24 us
  waiting for transfers between devices: 8.58 us -> 19.5 us
  matrix products: 19.4 us -> 26.3 us
  other arithmetic: 3 us -> 6.28 us
    all_gather x1 -> x0, blocking collectives: 32.7 us -> none  [on_device(): all_queries = lax.all_gather(own_queries, 'ctx', axis=0, tiled=True)]
    ppermute x0 -> x7, starting transfers between devices: none -> 15.6 us  [the longest x3 12.6 us: _cut_local_data(): oldest = lax.ppermute(oldest, axis_name=link_axis, perm=panels)]
    ppermute x0 -> x7, waiting for transfers between devices: none -> 10.9 us  [the longest x4 10.9 us: _cut_local_data(): arr_next = lax.ppermute(arr_next, link_axis, ledger)]
    dot_general x1 -> x8, matrix products: 2.69 us -> 9.7 us  [on_device(): jnp.einsum('rhc,tc->rht', part, prefix_cache, preferred_element_type=jnp....]
    all_to_all x1, blocking collectives: 11.8 us -> 8.85 us  [on_device(): lax.all_to_all(by_owner(row_mass), 'ctx', split_axis=0, concat_axis=0, ti...]
    reduce_max x0 -> x1, other arithmetic: none -> 1.84 us  [partial_stats(): row_peak = jnp.max(jnp.where(visible, scores, masked_value), axis=2)]
    unnamed x16 -> x21, local copies, waits for them, and re-layouts: 2.63 us -> 2.98 us
  transfers between devices with their start and end apart: 2 -> 9, of which waited for: 2 -> 6; matrix products, arithmetic and copies ran while one was open for 5% -> 13% of each run, Pallas kernels for 0% -> 0%
where the time goes in v1:
time: 132 us; the launch traced here: 131 us
  blocking collectives  49.7 us (38%)
  matrix products  26.3 us (20%)
  starting transfers between devices  24 us (18%)
  waiting for transfers between devices  19.5 us (15%)
  other arithmetic  6.28 us (5%)
  local copies, waits for them, and re-layouts  3.7 us (3%)
  between operations  1.55 us (1%)
    all_gather x1, blocking collectives, on_device(): every_value = lax.all_gather(flat_values, 'ctx', axis=0, tiled=True)  30.5 us
    ppermute x3, starting transfers between devices, _cut_local_data(): oldest = lax.ppermute(oldest, axis_name=link_axis, perm=panels)  12.6 us
    ppermute x4, waiting for transfers between devices, _cut_local_data(): arr_next = lax.ppermute(arr_next, link_axis, ledger)  10.9 us
    unnamed x1, blocking collectives  10.3 us
    dot_general x8, matrix products, on_device(): jnp.einsum('rhc,tc->rht', part, prefix_cache, preferred_element_type=jnp....  9.7 us
    all_to_all x1, blocking collectives, on_device(): lax.all_to_all(by_owner(row_mass), 'ctx', split_axis=0, concat_axis=0, ti...  8.85 us
    all_to_all x1, waiting for transfers between devices, on_device(): lax.all_to_all(by_owner(row_weighted), 'ctx', split_axis=0, concat_axis=0...  7.83 us
    dot_general x2, matrix products, partial_stats(): jnp.einsum(pattern, weights, values, preferred_element_type=jnp.float32)  5.87 us
  transfers between devices with their start and end apart: 9, of which 6 were waited for; matrix products, arithmetic and copies ran while one was open for 13% of the time, Pallas kernels for 0%

profile of v1, /device:TPU:0, one launch (start us, length us, event | category | flops | bytes accessed | tf_op | source)
XLA Modules:
  0.0 131.0 jit_solution(7794038126521634561)
XLA Ops:
  0.0 0.7 copy-done
  0.7 2.8 %fusion.27 = bf16[32,1,512]{2,1,0:T(2,128)(2,1)S(1)} fusion(bf16[32,128,512]{2,1,0:T(8,128)(2,1)} %param.12, bf16[32,128,1]{1,0,2:T(8,128)(2,1)S(1)} %bitcast.112), kind=kOutput, calls=%fused_computation.63 | convolution fusion | flops 4194304 | bytes 4235264 | tf_op jit(solution)/shard_map/rhn,hnc->rhc/dot_general | solution.py:60
  3.6 0.7 pad_maximum_fusion
  4.3 3.0 %collective-permute-start = (bf16[1,32,576]{2,1,0:T(8,128)(2,1)S(1)}, bf16[1,32,576]{2,1,0:T(8,128)(2,1)S(1)}, u32[]{:S(2)}, u32[]{:S(2)}) collective-permute-start(bf16[1,32,576]{2,1,0:T(8,128)(2,1)S(1)} %pad_maximum_fusion), channel_id=1, source_target_pairs={{0,4},{4,8},{8,12},{12,16},{16,20},{20,24},{24,28},{28,0},{1,5},{5... | collective-permute-start | bytes 110600 | tf_op jit(solution)/shard_map/ppermute | solution.py:26
  7.2 3.1 %collective-permute-start.4 = (bf16[1,32,576]{2,1,0:T(8,128)(2,1)S(1)}, bf16[1,32,576]{2,1,0:T(8,128)(2,1)S(1)}, u32[]{:S(2)}, u32[]{:S(2)}) collective-permute-start(bf16[1,32,576]{2,1,0:T(8,128)(2,1)S(1)} %pad_maximum_fusion), channel_id=1, source_target_pairs={{0,28},{4,0},{8,4},{12,8},{16,12},{20,16},{24,20},{28,24},{1,29},{... | collective-permute-start | bytes 110600 | tf_op jit(solution)/shard_map/ppermute | solution.py:30
  10.3 1.9 %collective-permute-done = bf16[1,32,576]{2,1,0:T(8,128)(2,1)S(1)} collective-permute-done((bf16[1,32,576]{2,1,0:T(8,128)(2,1)S(1)}, bf16[1,32,576]{2,1,0:T(8,128)(2,1)S(1)}, u32[]{:S(2)}, u32[]{:S(2)}) %collective-permute-start) | collective-permute-done | bytes 36896 | tf_op jit(solution)/shard_map/ppermute | solution.py:26
  12.2 0.7 broadcast_multiply_fusion
  12.9 6.0 %collective-permute-done.1 = bf16[1,32,576]{2,1,0:T(8,128)(2,1)S(1)} collective-permute-done((bf16[1,32,576]{2,1,0:T(8,128)(2,1)S(1)}, bf16[1,32,576]{2,1,0:T(8,128)(2,1)S(1)}, u32[]{:S(2)}, u32[]{:S(2)}) %collective-permute-start.1) | collective-permute-done | bytes 36896 | tf_op jit(solution)/shard_map/ppermute | solution.py:26
  18.9 0.1 iota_add_fusion
  19.0 0.1 add.49
  19.1 4.7 %collective-permute-start.5 = (bf16[1,32,576]{2,1,0:T(8,128)(2,1)S(1)}, bf16[1,32,576]{2,1,0:T(8,128)(2,1)S(1)}, u32[]{:S(2)}, u32[]{:S(2)}) collective-permute-start(bf16[1,32,576]{2,1,0:T(8,128)(2,1)S(1)} %collective-permute-done.4), channel_id=1, source_target_pairs={{0,28},{4,0},{8,4},{12,8},{16,12},{20,16},{24,20},{28,24},{1,29},{... | collective-permute-start | bytes 110600 | tf_op jit(solution)/shard_map/ppermute | solution.py:30
  23.8 1.8 %collective-permute-done.2 = bf16[1,32,576]{2,1,0:T(8,128)(2,1)S(1)} collective-permute-done((bf16[1,32,576]{2,1,0:T(8,128)(2,1)S(1)}, bf16[1,32,576]{2,1,0:T(8,128)(2,1)S(1)}, u32[]{:S(2)}, u32[]{:S(2)}) %collective-permute-start.2) | collective-permute-done | bytes 36896 | tf_op jit(solution)/shard_map/ppermute | solution.py:26
  25.6 0.7 broadcast_compare_fusion
  26.4 0.0 copy-start.1
  26.4 4.8 %collective-permute-start.6 = (bf16[1,32,576]{2,1,0:T(8,128)(2,1)S(1)}, bf16[1,32,576]{2,1,0:T(8,128)(2,1)S(1)}, u32[]{:S(2)}, u32[]{:S(2)}) collective-permute-start(bf16[1,32,576]{2,1,0:T(8,128)(2,1)S(1)} %collective-permute-done.5), channel_id=1, source_target_pairs={{0,28},{4,0},{8,4},{12,8},{16,12},{20,16},{24,20},{28,24},{1,29},{... | collective-permute-start | bytes 110600 | tf_op jit(solution)/shard_map/ppermute | solution.py:30
  31.2 1.1 collective-permute-done.3
  32.3 3.2 %constant_dynamic-update-slice_fusion.15 = (f32[16,32,4096]{2,1,0:T(8,128)S(1)}, f32[1,32,4096]{2,1,0:T(8,128)S(1)}) fusion(bf16[4096,576]{0,1:T(8,128)(2,1)} %param.15, bf16[1,32,576]{2,1,0:T(8,128)(2,1)S(1)} %collective-permute-done.3), kind=kOutput, calls=%fused_computation.57 | convolution fusion | flops 150994944 | bytes 5804032 | tf_op jit(solution)/shard_map/rhc,tc->rht/dot_general | solution.py:76
  35.6 0.9 constant_dynamic-update-slice_fusion.14
  36.5 0.0 copy-start.4
  36.5 0.9 constant_dynamic-update-slice_fusion.13
  37.5 0.9 constant_dynamic-update-slice_fusion.12
  38.4 0.0 copy-done.4
  38.4 0.9 constant_dynamic-update-slice_fusion.11
  39.3 0.9 constant_dynamic-update-slice_fusion.10
  40.3 0.9 constant_dynamic-update-slice_fusion.9
  41.2 0.0 collective-permute-done.6
  41.2 0.9 constant_dynamic-update-slice_fusion.8
  42.1 0.1 constant_dynamic-update-slice_fusion.7
  42.5 1.8 %select_reduce_fusion = f32[8,32]{1,0:T(8,128)} fusion(f32[16,32,4096]{2,1,0:T(8,128)S(1)} %constant_dynamic-update-slice_fusion, s32[]{:T(128)S(6)} %select_n.30, pred[8,4096]{1,0:T(8,128)(4,1)S(1)} %broadcast_compare_fusion), kind=kLoop, calls=%fused_computation.13 | loop fusion | flops 3145472 | bytes 4228100 | tf_op jit(solution)/shard_map/reduce_max | solution.py:36
  44.3 1.4 %copy-done.2 = f32[16,32,4096]{2,1,0:T(8,128)} copy-done((f32[16,32,4096]{2,1,0:T(8,128)}, f32[16,32,4096]{2,1,0:T(8,128)S(1)}, u32[]{:S(2)}) %copy-start.2) | copy-done | bytes 8388632
  45.7 1.9 %convert_reduce_fusion = f32[8,32]{1,0:T(8,128)S(1)} fusion(f32[8,32]{1,0:T(8,128)} %select_reduce_fusion, f32[16,32,4096]{2,1,0:T(8,128)S(1)} %constant_dynamic-update-slice_fusion, s32[]{:T(128)S(6)} %select_n.30, pred[8,4096]{1,0:T(8,128)(4,1)S(1)} %broadcast_compare_fusion), kind=kLoop, calls=%fused_computation.10 | loop fusion | flops 6291200 | bytes 4229124 | tf_op jit(solution)/shard_map/reduce_sum | solution.py:38
  47.6 8.8 %all_to_all.15 = f32[8,1,32]{2,1,0:T(1,128)S(1)} all-to-all(f32[8,1,32]{2,1,0:T(1,128)S(1)} %bitcast.118), channel_id=1, replica_groups=mesh['ctx'=8,'tp'=4] {'ctx'}, dimensions={0} | all-to-all | bytes 2048 | tf_op jit(solution)/shard_map/all_to_all | solution.py:101
  56.4 3.2 %all-to-all-start = ((f32[8,1,32]{2,1,0:T(1,128)}), f32[8,1,32]{2,1,0:T(1,128)S(1)}, u32[]{:S(2)}, u32[]{:S(2)}) async-start(f32[8,1,32]{2,1,0:T(1,128)} %bitcast.20), calls=%async_computation | async-start | bytes 8192 | tf_op jit(solution)/shard_map/all_to_all | solution.py:100
  59.7 0.0 copy-start.5
  59.7 5.7 %fusion.3 = f32[8,1,32,512]{3,2,1,0:T(8,128)} fusion(bf16[4096,576]{0,1:T(8,128)(2,1)} %param.15, f32[16,32,4096]{2,1,0:T(8,128)} %copy-done.2, s32[]{:T(128)S(6)} %select_n.30, f32[8,32]{1,0:T(8,128)} %select_reduce_fusion, pred[8,4096]{1,0:T(8,128)(4,1)S(1)} %broadcast_compare_fusion), kind=kOutput, calls=%fused_computation.15 | convolution fusion | flops 1077936128 | bytes 8949764 | tf_op jit(solution)/shard_map/rht,tc->rhc/dot_general | solution.py:39
  65.4 0.7 all-to-all-done
  66.1 5.2 %all-to-all-start.1 = ((f32[8,1,32,512]{3,2,1,0:T(8,128)}), f32[8,1,32,512]{3,2,1,0:T(8,128)S(1)}, u32[]{:S(2)}, u32[]{:S(2)}) async-start(f32[8,1,32,512]{3,2,1,0:T(8,128)} %fusion.3), calls=%async_computation.1 | async-start | bytes 1048576 | tf_op jit(solution)/shard_map/all_to_all | solution.py:102
  71.9 0.6 dynamic-slice
  73.2 0.3 select_reduce_fusion.1
  73.4 0.2 convert_reduce_fusion.1
  73.7 7.8 %all-to-all-done.1 = f32[8,1,32,512]{3,2,1,0:T(8,128)S(1)} async-done(((f32[8,1,32,512]{3,2,1,0:T(8,128)}), f32[8,1,32,512]{3,2,1,0:T(8,128)S(1)}, u32[]{:S(2)}, u32[]{:S(2)}) %all-to-all-start.1) | async-done | bytes 524320 | tf_op jit(solution)/shard_map/all_to_all | solution.py:102
  81.6 0.1 multiply_reduce_fusion
  81.7 0.2 fusion.8
  81.9 3.5 %fusion.15 = f32[32,1,128]{2,1,0:T(1,128)S(1)} fusion(bf16[32,512,128]{2,1,0:T(8,128)(2,1)} %param.13, f32[32,512,1]{1,0,2:T(8,128)S(1)} %fusion.8), kind=kOutput, calls=%fused_computation.29 | convolution fusion | flops 25165824 | bytes 4276224 | tf_op jit(solution)/shard_map/rhc,hcv->rhv/dot_general | solution.py:44
  85.4 30.5 %all-gather = bf16[8,1,4096]{2,1,0:T(2,128)(2,1)S(1)} all-gather(bf16[1,1,4096]{2,1,0:T(2,128)(2,1)S(1)} %reshape.203), channel_id=1, replica_groups=mesh['ctx'=8,'tp'=4] {'ctx'}, dimensions={0}, use_global_device_ids=true | all-gather | bytes 73728 | tf_op jit(solution)/shard_map/all_gather | solution.py:115
  115.9 4.1 %fusion.12 = f32[8,896]{1,0:T(8,128)S(1)} fusion(bf16[4096,896]{1,0:T(8,128)(2,1)} %param.14, bf16[8,1,4096]{2,1,0:T(2,128)(2,1)S(1)} %all-gather), kind=kOutput, calls=%fused_computation.25 | convolution fusion | flops 58720256 | bytes 7434240 | tf_op jit(solution)/shard_map/dot_general | solution.py:117
  120.1 10.3 %all-reduce = bf16[8,896]{1,0:T(8,128)(2,1)S(1)} all-reduce(f32[8,896]{1,0:T(8,128)S(1)} %fusion.12), channel_id=2, replica_groups=mesh['ctx'=8,'tp'=4] {'tp'}, use_global_device_ids=true, to_apply=%region_7.8.clone | all-reduce | flops 7168 | bytes 43008
  130.4 0.6 dynamic-slice_convert_fusion
  (26 shorter events, 0.4 us)
Async XLA Ops:
  0.0 0.7 copy-start
  4.3 8.0 %collective-permute-start = (bf16[1,32,576]{2,1,0:T(8,128)(2,1)S(1)}, bf16[1,32,576]{2,1,0:T(8,128)(2,1)S(1)}, u32[]{:S(2)}, u32[]{:S(2)}) collective-permute-start(bf16[1,32,576]{2,1,0:T(8,128)(2,1)S(1)} %pad_maximum_fusion), channel_id=1, source_target_pairs={{0,4},{4,8},{8,12},{12,16},{16,20},{20,24},{24,28},{28,0},{1,5},{5... | collective-permute-start | bytes 110600 | tf_op jit(solution)/shard_map/ppermute | solution.py:26
  7.2 11.9 %collective-permute-start.4 = (bf16[1,32,576]{2,1,0:T(8,128)(2,1)S(1)}, bf16[1,32,576]{2,1,0:T(8,128)(2,1)S(1)}, u32[]{:S(2)}, u32[]{:S(2)}) collective-permute-start(bf16[1,32,576]{2,1,0:T(8,128)(2,1)S(1)} %pad_maximum_fusion), channel_id=1, source_target_pairs={{0,28},{4,0},{8,4},{12,8},{16,12},{20,16},{24,20},{28,24},{1,29},{... | collective-permute-start | bytes 110600 | tf_op jit(solution)/shard_map/ppermute | solution.py:30
  12.2 6.7 %collective-permute-start.1 = (bf16[1,32,576]{2,1,0:T(8,128)(2,1)S(1)}, bf16[1,32,576]{2,1,0:T(8,128)(2,1)S(1)}, u32[]{:S(2)}, u32[]{:S(2)}) collective-permute-start(bf16[1,32,576]{2,1,0:T(8,128)(2,1)S(1)} %collective-permute-done), channel_id=1, source_target_pairs={{0,4},{4,8},{8,12},{12,16},{16,20},{20,24},{24,28},{28,0},{1,5},{5... | collective-permute-start | bytes 110600 | tf_op jit(solution)/shard_map/ppermute | solution.py:26
  18.9 6.7 %collective-permute-start.2 = (bf16[1,32,576]{2,1,0:T(8,128)(2,1)S(1)}, bf16[1,32,576]{2,1,0:T(8,128)(2,1)S(1)}, u32[]{:S(2)}, u32[]{:S(2)}) collective-permute-start(bf16[1,32,576]{2,1,0:T(8,128)(2,1)S(1)} %collective-permute-done.1), channel_id=1, source_target_pairs={{0,4},{4,8},{8,12},{12,16},{16,20},{20,24},{24,28},{28,0},{1,5},{5... | collective-permute-start | bytes 110600 | tf_op jit(solution)/shard_map/ppermute | solution.py:26
  19.1 7.3 %collective-permute-start.5 = (bf16[1,32,576]{2,1,0:T(8,128)(2,1)S(1)}, bf16[1,32,576]{2,1,0:T(8,128)(2,1)S(1)}, u32[]{:S(2)}, u32[]{:S(2)}) collective-permute-start(bf16[1,32,576]{2,1,0:T(8,128)(2,1)S(1)} %collective-permute-done.4), channel_id=1, source_target_pairs={{0,28},{4,0},{8,4},{12,8},{16,12},{20,16},{24,20},{28,24},{1,29},{... | collective-permute-start | bytes 110600 | tf_op jit(solution)/shard_map/ppermute | solution.py:30
  25.6 6.7 %collective-permute-start.3 = (bf16[1,32,576]{2,1,0:T(8,128)(2,1)S(1)}, bf16[1,32,576]{2,1,0:T(8,128)(2,1)S(1)}, u32[]{:S(2)}, u32[]{:S(2)}) collective-permute-start(bf16[1,32,576]{2,1,0:T(8,128)(2,1)S(1)} %collective-permute-done.2), channel_id=1, source_target_pairs={{0,4},{4,8},{8,12},{12,16},{16,20},{20,24},{24,28},{28,0},{1,5},{5... | collective-permute-start | bytes 110600 | tf_op jit(solution)/shard_map/ppermute | solution.py:26
  26.4 9.2 %copy-start.1 = (bf16[4096,576]{0,1:T(8,128)(2,1)S(1)}, bf16[4096,576]{0,1:T(8,128)(2,1)}, u32[]{:S(2)}) copy-start(bf16[4096,576]{0,1:T(8,128)(2,1)} %param.15) | copy-start | bytes 14155780
  26.4 14.8 %collective-permute-start.6 = (bf16[1,32,576]{2,1,0:T(8,128)(2,1)S(1)}, bf16[1,32,576]{2,1,0:T(8,128)(2,1)S(1)}, u32[]{:S(2)}, u32[]{:S(2)}) collective-permute-start(bf16[1,32,576]{2,1,0:T(8,128)(2,1)S(1)} %collective-permute-done.5), channel_id=1, source_target_pairs={{0,28},{4,0},{8,4},{12,8},{16,12},{20,16},{24,20},{28,24},{1,29},{... | collective-permute-start | bytes 110600 | tf_op jit(solution)/shard_map/ppermute | solution.py:30
  36.5 1.9 %copy-start.4 = (bf16[1,32,64]{2,1,0:T(8,128)(2,1)S(1)}, bf16[1,32,64]{2,1,0:T(8,128)(2,1)}, u32[]{:S(2)}) copy-start(bf16[1,32,64]{2,1,0:T(8,128)(2,1)} %param.11) | copy-start | bytes 12292
  42.5 3.2 %copy-start.2 = (f32[16,32,4096]{2,1,0:T(8,128)}, f32[16,32,4096]{2,1,0:T(8,128)S(1)}, u32[]{:S(2)}) copy-start(f32[16,32,4096]{2,1,0:T(8,128)S(1)} %constant_dynamic-update-slice_fusion) | copy-start | bytes 25165828
  56.4 9.7 %all-to-all-start = ((f32[8,1,32]{2,1,0:T(1,128)}), f32[8,1,32]{2,1,0:T(1,128)S(1)}, u32[]{:S(2)}, u32[]{:S(2)}) async-start(f32[8,1,32]{2,1,0:T(1,128)} %bitcast.20), calls=%async_computation | async-start | bytes 8192 | tf_op jit(solution)/shard_map/all_to_all | solution.py:100
  59.7 12.3 %copy-start.5 = (u32[32]{0:T(128)S(1)}, u32[32]{0:T(128)}, u32[]{:S(2)}) copy-start(u32[32]{0:T(128)} %constant.48) | copy-start | bytes 388
  59.7 13.5 %copy-start.3 = (bf16[1,256,576]{1,2,0:T(8,128)(2,1)S(1)}, bf16[1,256,576]{1,2,0:T(8,128)(2,1)}, u32[]{:S(2)}) copy-start(bf16[1,256,576]{1,2,0:T(8,128)(2,1)} %param.18) | copy-start | bytes 884740
  66.1 15.5 %all-to-all-start.1 = ((f32[8,1,32,512]{3,2,1,0:T(8,128)}), f32[8,1,32,512]{3,2,1,0:T(8,128)S(1)}, u32[]{:S(2)}, u32[]{:S(2)}) async-start(f32[8,1,32,512]{3,2,1,0:T(8,128)} %fusion.3), calls=%async_computation.1 | async-start | bytes 1048576 | tf_op jit(solution)/shard_map/all_to_all | solution.py:102
